TPU v7x, 32 devices: a whole 2x2x4 slice. The times are simulated.
32 devices in a mesh: rep: 2 (over core), space: 16 (over z, y, x).
Axes of the slice: x: 2, y: 2, z: 4, core: 2. Of those that a mesh axis runs over, the one named last changes fastest.
Arguments:
- particles: float32 [6, 2, 8192, 128], P(None, 'rep', 'space'), may hold values from -6 to 6
- pair_order: int32 [2, 8192, 128], P('rep', 'space'), may hold values from 0 to 127, each once within a row
- accepted: int32 [2, 8192, 64], P('rep', 'space'), may hold values 0 or 1
- direction: int32 [2, 8192, 64], P('rep', 'space'), may hold values from 0 to 255
- destination: int32 [2, 8192], P('rep', 'space'), may hold values from 0 to 15, as said below
- live_count: int32 [2, 16], P('rep', 'space'), may hold values from 256 to 512, as said below
- cell_index: int32 [2, 8192], P('rep', 'space'), may hold values from 0 to 255
Outputs:
- moved: float32 [6, 2, 12288, 128], P(None, 'rep', 'space')
- samples: float32 [4, 16, 256], P(None, 'space', 'rep')
Inputs may be any that keep to these rules, and one draw needn't show every extreme that they name: Every block's destination is its own slab or one of the two beside it, slab 0 and slab 16 - 1 being beside each other; only live blocks leave; one slab of one replica sends at most 128 blocks to each of its two neighbours, and in every replica some slab sends exactly 128 to its upper and some slab exactly 128 to its lower neighbour. `live_count`: the count of live blocks of each slab of each replica; slab 0 of replica 0 is full.
All inputs are finite; a program needn't handle non-finite values. No bound on the sum of `accepted` on one device may be relied on, other than what follows from the above.
Results may differ from a plain program's by a relative error of at most 0.0003.
Values sent between devices are 32-bit elements; how exact they have to be, the bound alone decides.
A program may use at most 64 MiB of HBM per device.

v0:
```python
import functools

import jax
import jax.numpy as jnp
from jax import lax
from jax.experimental import pallas as pl
from jax.experimental.pallas import tpu as pltpu
from jax.sharding import PartitionSpec as P

NDIR = 256
MOVE = 128
CELLS = 256
TIME_STEP = 0.25
GOLDEN_TURN = 2.399963229728653
ROWS = 128


def take_lanes(values, index):
    return jnp.take_along_axis(values, index, axis=1, mode="promise_in_bounds")


def split3(value):
    high = value.astype(jnp.bfloat16)
    rest = value - high.astype(jnp.float32)
    middle = rest.astype(jnp.bfloat16)
    low = (rest - middle.astype(jnp.float32)).astype(jnp.bfloat16)
    return high, middle, low


def dot(left, right):
    return jnp.dot(left, right, preferred_element_type=jnp.float32)


def dot_nt(left, right):
    return lax.dot_general(left, right, (((1,), (1,)), ((), ())), preferred_element_type=jnp.float32)


def inverse_order(order):
    chunk, part = order.shape
    count = part // 8
    lane = lax.broadcasted_iota(jnp.int32, (chunk, part), 1)
    keys = jnp.transpose((order * part + lane).astype(jnp.float32))
    rows = [keys[8 * i:8 * i + 8] for i in range(count)]
    sublane = lax.broadcasted_iota(jnp.int32, (8, chunk), 0)
    sign = None
    size = 2
    while size <= part:
        wanted = None
        if count <= size < part:
            wanted = jnp.where((sublane & (size // count)) == 0, 1.0, -1.0)
        if sign is not None or wanted is not None:
            flip = wanted if sign is None else sign if wanted is None else sign * wanted
            rows = [row * flip for row in rows]
        sign = wanted
        stride = size // 2
        while stride >= 1:
            if stride >= count:
                apart = stride // count
                is_low = (sublane & apart) == 0
                swapped = [jnp.take_along_axis(row, sublane ^ apart, axis=0, mode="promise_in_bounds") for row in rows]
                rows = [jnp.where(is_low, jnp.minimum(r, o), jnp.maximum(r, o)) for r, o in zip(rows, swapped)]
            else:
                after = list(rows)
                for i in range(count):
                    j = i ^ stride
                    rising = size >= count or (i & size) == 0
                    pick = jnp.minimum if (i < j) == rising else jnp.maximum
                    after[i] = pick(rows[i], rows[j])
                rows = after
            stride //= 2
        size *= 2
    ranked = [(row - ((sublane * count + i) * part).astype(jnp.float32)) for i, row in enumerate(rows)]
    placed = jnp.transpose(jnp.concatenate(ranked, axis=0)).astype(jnp.int32)
    return take_lanes(placed, (lane & (count - 1)) * 8 + lane // count)


def pick_rows(chosen, pieces):
    return dot(chosen, pieces[0]) + dot(chosen, pieces[1]) + dot(chosen, pieces[2])


def one_hot_rows(slots, cap):
    slot = lax.broadcasted_iota(jnp.int32, (MOVE, cap), 0)
    return jnp.concatenate(
        [jnp.where(slot == slots[j:j + 1, :], 1.0, 0.0) for j in range(2)], axis=0
    ).astype(jnp.bfloat16)


def mover_slots(dest, living, upper_slab, lower_slab):
    cap = dest.shape[1]
    chunk = MOVE
    leaving = [living & (dest == upper_slab), living & (dest == lower_slab)]
    flags = jnp.concatenate([jnp.where(m, 1.0, 0.0) for m in leaving], axis=0)
    triangle = (
        lax.broadcasted_iota(jnp.int32, (chunk, chunk), 0) <= lax.broadcasted_iota(jnp.int32, (chunk, chunk), 1)
    )
    triangle = jnp.where(triangle, 1.0, 0.0).astype(jnp.bfloat16)
    before = jnp.zeros((2, 1), jnp.float32)
    ranks = []
    for i in range(cap // chunk):
        piece = flags[:, i * chunk:(i + 1) * chunk]
        inside = dot(piece.astype(jnp.bfloat16), triangle)
        ranks.append(inside + before)
        before = before + inside[:, chunk - 1:chunk]
    ranking = jnp.concatenate(ranks, axis=1)
    return jnp.where(flags > 0.0, ranking - 1.0, -1.0).astype(jnp.int32)


def main_kernel(slabs, steps, part_ref, order_ref, flag_ref, turn_ref, dest_ref, live_ref, cell_ref, place_ref,
                moved_ref, samples_ref, table, packed_t, keep_t, inverse_t, parts, square, slot_ref,
                sent_place, sent_speed, got_place, got_speed, sent_cells, got_cells, send_sem, recv_sem):
    step = pl.program_id(0)
    chunk, part = order_ref.shape
    pairs = part // 2
    cap = dest_ref.shape[1]
    reps, _, share = sent_cells.shape
    my_slab = lax.axis_index("space")
    my_rep = lax.axis_index("rep")
    upper_slab = lax.rem(my_slab + 1, slabs)
    lower_slab = lax.rem(my_slab + slabs - 1, slabs)
    goals = (upper_slab, lower_slab)

    def copy(source, target, k, device):
        return pltpu.make_async_remote_copy(
            src_ref=source, dst_ref=target, send_sem=send_sem.at[k], recv_sem=recv_sem.at[k],
            device_id=device, device_id_type=pl.DeviceIdType.MESH,
        )

    place_copies, speed_copies = [
        [[copy(sent.at[j, k], got.at[j, k], base + 3 * j + k, {"space": goals[j]}) for k in range(3)] for j in range(2)]
        for sent, got, base in ((sent_place, got_place, 0), (sent_speed, got_speed, 6))
    ]
    cell_copies = [
        copy(sent_cells.at[k], got_cells.at[k], 11 + k, {"rep": lax.rem(my_rep + k, reps)}) for k in range(1, reps)
    ]

    @pl.when(step == 0)
    def _():
        barrier = pltpu.get_barrier_semaphore()
        for j in range(2):
            pl.semaphore_signal(barrier, inc=1, device_id={"space": goals[j]}, device_id_type=pl.DeviceIdType.MESH)
        for k in range(1, reps):
            pl.semaphore_signal(
                barrier, inc=1, device_id={"rep": lax.rem(my_rep + k, reps)}, device_id_type=pl.DeviceIdType.MESH
            )
        living = lax.broadcasted_iota(jnp.int32, (1, cap), 1) < live_ref[...]
        slots = mover_slots(dest_ref[...], living, upper_slab, lower_slab)
        slot_ref[...] = slots
        chosen = one_hot_rows(slots, cap)
        for k in range(3):
            sent = pick_rows(chosen, split3(place_ref[k]))
            sent_place[0, k] = sent[:MOVE]
            sent_place[1, k] = sent[MOVE:]
            if k == 0:
                pl.semaphore_wait(barrier, 1 + reps)
            for j in range(2):
                place_copies[j][k].start()

    @pl.when(step == 0)
    def _():
        for half in range(2):
            turns = (lax.broadcasted_iota(jnp.int32, (8, part), 1) + half * part).astype(jnp.float32)
            height = 1.0 - (2.0 * turns + 1.0) / NDIR
            radius = jnp.sqrt(1.0 - height * height)
            angle = turns * GOLDEN_TURN
            table[half] = radius * jnp.cos(angle)
            table[half + 2] = radius * jnp.sin(angle)

    @pl.when(step < steps)
    def _():
        pair_code = turn_ref[...] + NDIR * flag_ref[...]
        packed_t[...] = jnp.transpose(jnp.concatenate([pair_code, pair_code], axis=0))
        start = pl.multiple_of(step * chunk, chunk)
        slots = lax.broadcasted_iota(jnp.int32, (1, chunk), 1) + step * chunk
        staying = (dest_ref[:, pl.ds(start, chunk)] == my_slab) & (slots < live_ref[...])
        stay_rows = jnp.broadcast_to(jnp.where(staying, 1.0, 0.0), (part, chunk))
        keep_t[...] = jnp.transpose(stay_rows)
        inverse_t[...] = inverse_order(order_ref[...])

        def rows_step(i, carry):
            row = pl.multiple_of(i * ROWS, ROWS)
            here = pl.ds(row, ROWS)
            order = order_ref[here, :]
            inverse = inverse_t[here, :]
            partner = take_lanes(order, inverse ^ pairs)
            code = take_lanes(packed_t[here, :], inverse & (pairs - 1))
            taken = code >= NDIR
            turn = code & (NDIR - 1)
            low_index = turn & (part - 1)
            is_high = turn >= part
            wide = (ROWS, part)
            tables = [jnp.broadcast_to(table[k, 0:1, :], wide) for k in range(4)]
            unit_x = jnp.where(is_high, take_lanes(tables[1], low_index), take_lanes(tables[0], low_index))
            unit_y = jnp.where(is_high, take_lanes(tables[3], low_index), take_lanes(tables[2], low_index))
            unit_z = 1.0 - (2.0 * turn.astype(jnp.float32) + 1.0) / NDIR
            old = [part_ref[3 + k, here, :] for k in range(3)]
            other = [take_lanes(v, partner) for v in old]
            relative = [a - b for a, b in zip(old, other)]
            speed = jnp.sqrt(relative[0] * relative[0] + relative[1] * relative[1] + relative[2] * relative[2])
            half_speed = jnp.where(inverse < pairs, 0.5, -0.5) * speed
            new = [
                jnp.where(taken, 0.5 * (a + b) + half_speed * u, a)
                for a, b, u in zip(old, other, (unit_x, unit_y, unit_z))
            ]
            keep = keep_t[here, :] > 0.0
            target = pl.ds(pl.multiple_of(MOVE + step * chunk + row, ROWS), ROWS)
            block = pl.ds(pl.multiple_of(step * chunk + row, ROWS), ROWS)
            square[block, :] = new[0] * new[0] + new[1] * new[1] + new[2] * new[2]
            for k in range(3):
                moved_ref[k, target, :] = jnp.where(keep, part_ref[k, here, :] + TIME_STEP * new[k], 0.0)
                moved_ref[3 + k, target, :] = jnp.where(keep, new[k], 0.0)
                for j, piece in enumerate(split3(new[k])):
                    parts[j, block, pl.ds(k * part, part)] = piece
            return carry

        lax.fori_loop(0, chunk // ROWS, rows_step, 0)

    @pl.when(step == steps - 1)
    def _():
        chosen = one_hot_rows(slot_ref[...], cap)
        for k in range(3):
            sent = pick_rows(chosen, [parts[j, :, pl.ds(k * part, part)] for j in range(3)])
            sent_speed[0, k] = sent[:MOVE]
            sent_speed[1, k] = sent[MOVE:]
            for j in range(2):
                speed_copies[j][k].start()

        living = lax.broadcasted_iota(jnp.int32, (1, cap), 1) < live_ref[...]
        ones = jnp.ones((8, part), jnp.bfloat16)
        eight = lax.broadcasted_iota(jnp.int32, (8, cap), 0)
        terms = []
        for k in range(3):
            here = pl.ds(k * part, part)
            terms.append(dot_nt(ones, parts[0, :, here]) + dot_nt(ones, parts[1, :, here]) + dot_nt(ones, parts[2, :, here]))
        pieces = split3(square[...])
        terms.append(dot_nt(ones, pieces[0]) + dot_nt(ones, pieces[1]) + dot_nt(ones, pieces[2]))
        term = jnp.where(eight == 0, terms[0], jnp.where(eight == 1, terms[1], jnp.where(eight == 2, terms[2], terms[3])))
        term = jnp.where(living, term, 0.0)
        shifted = cell_ref[...] + (CELLS - my_rep * share)
        shifted = jnp.where(shifted >= CELLS, shifted - CELLS, shifted)
        cells = lax.broadcasted_iota(jnp.int32, (CELLS, cap), 0)
        in_cell = jnp.where(cells == shifted, 1.0, 0.0).astype(jnp.bfloat16)
        high, middle, low = split3(term)
        total = dot_nt(high, in_cell) + dot_nt(middle, in_cell) + dot_nt(low, in_cell)
        for j in range(reps):
            sent_cells[j] = total[0:4, j * share:(j + 1) * share]
        for each in cell_copies:
            each.start()

        total = sent_cells[0]
        for k in range(1, reps):
            cell_copies[k - 1].wait()
            total = total + got_cells[k]
        samples_ref[...] = total / (part * reps)
        for k in range(3):
            for j, at in ((0, 0), (1, MOVE + cap)):
                target = pl.ds(at, MOVE)
                place_copies[j][k].wait()
                speed_copies[j][k].wait()
                moved_ref[k, target, :] = got_place[j, k] + TIME_STEP * got_speed[j, k]
                moved_ref[3 + k, target, :] = got_speed[j, k]


def per_device(particles, pair_order, accepted, direction, destination, live_count, cell_index):
    six, _, cap, part = particles.shape
    three = six // 2
    pairs = accepted.shape[2]
    chunk = MOVE
    steps = cap // chunk
    slabs = lax.axis_size("space")
    reps = lax.axis_size("rep")
    share = CELLS // reps
    f32 = jnp.float32
    out_cap = cap + 2 * MOVE
    current = particles.reshape(six, cap, part)
    call = pl.pallas_call(
        functools.partial(main_kernel, slabs, steps),
        grid=(steps,),
        in_specs=[
            pl.BlockSpec((six, chunk, part), lambda i: (0, i, 0)),
            pl.BlockSpec((chunk, part), lambda i: (i, 0)),
            pl.BlockSpec((pairs, chunk), lambda i: (0, i)),
            pl.BlockSpec((pairs, chunk), lambda i: (0, i)),
            pl.BlockSpec((1, cap), lambda i: (0, 0)),
            pl.BlockSpec((1, 1), lambda i: (0, 0)),
            pl.BlockSpec((1, cap), lambda i: (0, 0)),
            pl.BlockSpec((three, cap, part), lambda i: (0, 0, 0)),
        ],
        out_specs=[
            pl.BlockSpec(memory_space=pltpu.VMEM),
            pl.BlockSpec((4, share), lambda i: (0, 0)),
        ],
        out_shape=[
            jax.ShapeDtypeStruct((six, out_cap, part), f32),
            jax.ShapeDtypeStruct((4, share), f32),
        ],
        scratch_shapes=[
            pltpu.VMEM((4, 8, part), f32),
            pltpu.VMEM((chunk, part), jnp.int32),
            pltpu.VMEM((chunk, part), f32),
            pltpu.VMEM((chunk, part), jnp.int32),
            pltpu.VMEM((3, cap, three * part), jnp.bfloat16),
            pltpu.VMEM((cap, part), f32),
            pltpu.VMEM((2, cap), jnp.int32),
            pltpu.VMEM((2, three, MOVE, part), f32),
            pltpu.VMEM((2, three, MOVE, part), f32),
            pltpu.VMEM((2, three, MOVE, part), f32),
            pltpu.VMEM((2, three, MOVE, part), f32),
            pltpu.VMEM((reps, 4, share), f32),
            pltpu.VMEM((reps, 4, share), f32),
            pltpu.SemaphoreType.DMA((11 + reps,)),
            pltpu.SemaphoreType.DMA((11 + reps,)),
        ],
        compiler_params=pltpu.CompilerParams(collective_id=0, has_side_effects=True, vmem_limit_bytes=16 * 2 ** 20),
        name="step",
    )
    operands = (
        current,
        pair_order.reshape(cap, part),
        jnp.transpose(accepted.reshape(cap, pairs)),
        jnp.transpose(direction.reshape(cap, pairs)),
        destination.reshape(1, cap),
        live_count,
        cell_index.reshape(1, cap),
        current,
    )
    hold = functools.partial(pltpu.with_memory_space_constraint, memory_space=pltpu.HBM)
    operands = [x if x is live_count else hold(x) for x in operands]
    moved, samples = call(*operands)
    return (moved[:, None], samples[:, None, :])


def solution(mesh):
    return jax.shard_map(
        per_device,
        mesh=mesh,
        in_specs=(
            P(None, "rep", "space", None),
            P("rep", "space", None),
            P("rep", "space", None),
            P("rep", "space", None),
            P("rep", "space"),
            P("rep", "space"),
            P("rep", "space"),
        ),
        out_specs=(P(None, "rep", "space", None), P(None, "space", "rep")),
        check_vma=False,
    )
```

profile of v0, /device:TPU:0, one launch (start us, length us, event | category | flops | bytes accessed | tf_op | source)
XLA Modules:
  0.0 26.7 jit_solution(18139167749214956153)
XLA Ops:
  1.3 23.4 %step.1 = (f32[6,768,128]{2,1,0:T(8,128)S(1)}, f32[4,128]{1,0:T(4,128)S(1)}) custom-call(f32[6,512,128]{2,1,0:T(8,128)} %bitcast.16, s32[512,128]{1,0:T(8,128)} %bitcast.18, s32[64,512]{1,0:T(8,128)} %bitcast.19, s32[64,512]{1,0:T(8,128)} %bitcast.20, s32[1,512]{1,0:T(1,128)} %dest_ref.1, s32[1,1]{1,0:T(1,128)S(6)} %copy.13.live_ref, s32[1,512]{1,0:T(1,128)} %cell_ref.1, ...), custom_call_target="tpu_custom_call" | custom-call | tf_op jit(solution)/shard_map/step/pallas_call | solution.py:328
  24.7 1.4 %copy.14 = f32[6,1,768,128]{3,2,1,0:T(8,128)} copy(f32[6,1,768,128]{3,2,1,0:T(8,128)S(1)} %bitcast.14) | data formatting | bytes 4718592
  26.1 0.6 %copy.15 = f32[4,1,128]{2,1,0:T(1,128)} copy(f32[4,1,128]{2,1,0:T(1,128)S(1)} %bitcast.15) | data formatting | bytes 4096
where the time goes:
time: 26.9 us; the launch traced here: 26.7 us
  Pallas kernels  23.4 us (87%)
  local copies, waits for them, and re-layouts  1.99 us (7%)
  between operations  1.29 us (5%)
    pallas_call x1, Pallas kernels, per_device(): moved, samples = call(*operands)  23.4 us
    unnamed x2, local copies, waits for them, and re-layouts  1.99 us

commit v1 on v0

v1 whole, which is shorter than its diff:
```python
import functools

import jax
import jax.numpy as jnp
from jax import lax
from jax.experimental import pallas as pl
from jax.experimental.pallas import tpu as pltpu
from jax.sharding import PartitionSpec as P

NDIR = 256
MOVE = 128
CELLS = 256
TIME_STEP = 0.25
GOLDEN_TURN = 2.399963229728653


def take_lanes(values, index):
    return jnp.take_along_axis(values, index, axis=1, mode="promise_in_bounds")


def split3(value):
    high = value.astype(jnp.bfloat16)
    rest = value - high.astype(jnp.float32)
    middle = rest.astype(jnp.bfloat16)
    low = (rest - middle.astype(jnp.float32)).astype(jnp.bfloat16)
    return high, middle, low


def split2(value):
    high = value.astype(jnp.bfloat16)
    return high, (value - high.astype(jnp.float32)).astype(jnp.bfloat16)


def dot(left, right):
    return jnp.dot(left, right, preferred_element_type=jnp.float32)


def dot_nt(left, right):
    return lax.dot_general(left, right, (((1,), (1,)), ((), ())), preferred_element_type=jnp.float32)


def inverse_order(order):
    chunk, part = order.shape
    count = part // 8
    lane = lax.broadcasted_iota(jnp.int32, (chunk, part), 1)
    keys = jnp.transpose((order * part + lane).astype(jnp.float32))
    rows = [keys[8 * i:8 * i + 8] for i in range(count)]
    sublane = lax.broadcasted_iota(jnp.int32, (8, chunk), 0)
    sign = None
    size = 2
    while size <= part:
        wanted = None
        if count <= size < part:
            wanted = jnp.where((sublane & (size // count)) == 0, 1.0, -1.0)
        if sign is not None or wanted is not None:
            flip = wanted if sign is None else sign if wanted is None else sign * wanted
            rows = [row * flip for row in rows]
        sign = wanted
        stride = size // 2
        while stride >= 1:
            if stride >= count:
                apart = stride // count
                is_low = (sublane & apart) == 0
                swapped = [jnp.take_along_axis(row, sublane ^ apart, axis=0, mode="promise_in_bounds") for row in rows]
                rows = [jnp.where(is_low, jnp.minimum(r, o), jnp.maximum(r, o)) for r, o in zip(rows, swapped)]
            else:
                after = list(rows)
                for i in range(count):
                    j = i ^ stride
                    rising = size >= count or (i & size) == 0
                    pick = jnp.minimum if (i < j) == rising else jnp.maximum
                    after[i] = pick(rows[i], rows[j])
                rows = after
            stride //= 2
        size *= 2
    ranked = [(row - ((sublane * count + i) * part).astype(jnp.float32)) for i, row in enumerate(rows)]
    placed = jnp.transpose(jnp.concatenate(ranked, axis=0)).astype(jnp.int32)
    return take_lanes(placed, (lane & (count - 1)) * 8 + lane // count)


def pick_rows(chosen, pieces):
    part = pieces[0].shape[1]
    both = dot(chosen, jnp.concatenate(pieces, axis=1))
    return both[:, :part] + both[:, part:]


def choose_movers(dest_ref, live, goals, chosen_ref):
    cap = dest_ref.shape[1]
    chunk = MOVE
    count = cap // chunk
    lane = lax.broadcasted_iota(jnp.int32, (1, chunk), 1)
    flags = []
    for goal in goals:
        for i in range(count):
            here = dest_ref[:, i * chunk:(i + 1) * chunk]
            flags.append(jnp.where((here == goal) & (lane + i * chunk < live), 1.0, 0.0))
    flags = jnp.concatenate(flags, axis=0)
    row = lax.broadcasted_iota(jnp.int32, (chunk, 2 * chunk), 0)
    column = lax.broadcasted_iota(jnp.int32, (chunk, 2 * chunk), 1)
    sums = jnp.where((row <= column), 1.0, 0.0).astype(jnp.bfloat16)
    counted = dot(flags.astype(jnp.bfloat16), sums)
    slot = lax.broadcasted_iota(jnp.int32, (chunk, chunk), 0)
    for j in range(2):
        before = jnp.zeros((1, chunk), jnp.float32)
        for i in range(count):
            at = j * count + i
            rank = counted[at:at + 1, :chunk] + before
            place = jnp.where(flags[at:at + 1] > 0.0, rank - 1.0, -1.0).astype(jnp.int32)
            chosen_ref[pl.ds(j * MOVE, MOVE), pl.ds(i * chunk, chunk)] = jnp.where(slot == place, 1.0, 0.0).astype(jnp.bfloat16)
            before = before + counted[at:at + 1, chunk:]


def main_kernel(slabs, part_hbm, order_hbm, flag_hbm, turn_hbm, dest_hbm, live_ref, cell_hbm,
                moved_ref, samples_ref, part_ref, order_ref, flag_ref, turn_ref, dest_ref, cell_ref,
                table, packed_t, keep_t, inverse_t, parts, square, chosen_ref,
                sent_place, sent_speed, got_place, got_speed, sent_cells, got_cells,
                load_sem, send_sem, recv_sem, far_sem):
    cap, part = order_ref.shape
    chunk = MOVE
    steps = cap // chunk
    pairs = part // 2
    reps, _, share = sent_cells.shape
    my_slab = lax.axis_index("space")
    my_rep = lax.axis_index("rep")
    odd = lax.rem(my_slab, 2)
    near = odd
    far = 1 - odd
    near_slab = my_slab + 1 - 2 * odd
    far_slab = lax.rem(my_slab + slabs - 1 + 2 * odd, slabs)
    goals = (lax.rem(my_slab + 1, slabs), lax.rem(my_slab + slabs - 1, slabs))
    is_end = (my_slab == 0) | (my_slab == slabs - 1)
    middle = slabs // 2 - 1
    is_middle = my_slab == middle
    is_first = my_slab == 1
    live = live_ref[0, 0]

    loads = []

    def load(source, target):
        each = pltpu.make_async_copy(source, target, load_sem.at[len(loads)])
        each.start()
        loads.append(each)
        return each

    dest_load = load(dest_hbm, dest_ref)
    place_loads = [load(part_hbm.at[k], part_ref.at[k]) for k in range(3)]
    turn_load = load(turn_hbm, turn_ref)
    flag_load = load(flag_hbm, flag_ref)
    order_load = load(order_hbm, order_ref)
    speed_load = load(part_hbm.at[pl.ds(3, 3)], part_ref.at[pl.ds(3, 3)])
    cell_load = load(cell_hbm, cell_ref)

    def copy(source, target, k, device):
        return pltpu.make_async_remote_copy(
            src_ref=source, dst_ref=target, send_sem=send_sem.at[k], recv_sem=recv_sem.at[k],
            device_id=device, device_id_type=pl.DeviceIdType.MESH,
        )

    def mover_copies(sent, got, base, j, device):
        return [copy(sent.at[j, k], got.at[j, k], base + 3 * j + k, {"space": device}) for k in range(3)]

    place_far = mover_copies(sent_place, got_place, 0, far, far_slab)
    place_near = mover_copies(sent_place, got_place, 0, near, near_slab)
    speed_far = mover_copies(sent_speed, got_speed, 6, far, far_slab)
    speed_near = mover_copies(sent_speed, got_speed, 6, near, near_slab)
    cell_copies = [
        copy(sent_cells.at[k], got_cells.at[k], 11 + k, {"rep": lax.rem(my_rep + k, reps)}) for k in range(1, reps)
    ]

    def start(copies):
        for each in copies:
            each.start()

    barrier = pltpu.get_barrier_semaphore()

    def greet(**device):
        pl.semaphore_signal(barrier, inc=1, device_id=device, device_id_type=pl.DeviceIdType.MESH)

    greet(space=near_slab)
    for k in range(1, reps):
        greet(rep=lax.rem(my_rep + k, reps))

    @pl.when(is_end)
    def _():
        greet(space=middle)

    @pl.when(jnp.logical_not(is_end))
    def _():
        greet(space=far_slab)

    dest_load.wait()
    choose_movers(dest_ref, live, goals, chosen_ref)
    for k in range(3):
        place_loads[k].wait()
        sent = pick_rows(chosen_ref[...], split2(part_ref[k]))
        sent_place[0, k] = sent[:MOVE]
        sent_place[1, k] = sent[MOVE:]
        if k == 0:
            @pl.when(is_end)
            def _():
                pl.semaphore_wait(barrier, reps)

            @pl.when(is_middle)
            def _():
                pl.semaphore_wait(barrier, 3 + reps)
                for end in (0, slabs - 1):
                    pl.semaphore_signal(far_sem, inc=1, device_id={"space": end}, device_id_type=pl.DeviceIdType.MESH)

            @pl.when(jnp.logical_not(is_end | is_middle))
            def _():
                pl.semaphore_wait(barrier, 1 + reps)

        @pl.when(jnp.logical_not(is_end | is_first))
        def _(k=k):
            place_far[k].start()

        place_near[k].start()

        @pl.when(is_first)
        def _(k=k):
            place_far[k].start()

    for half in range(2):
        turns = (lax.broadcasted_iota(jnp.int32, (8, part), 1) + half * part).astype(jnp.float32)
        height = 1.0 - (2.0 * turns + 1.0) / NDIR
        radius = jnp.sqrt(1.0 - height * height)
        angle = turns * GOLDEN_TURN
        table[half] = radius * jnp.cos(angle)
        table[half + 2] = radius * jnp.sin(angle)

    turn_load.wait()
    flag_load.wait()
    order_load.wait()
    speed_load.wait()

    def chunk_step(step, carry):
        at = pl.multiple_of(step * chunk, chunk)
        here = pl.ds(at, chunk)
        pair_code = turn_ref[:, here] + NDIR * flag_ref[:, here]
        packed_t[...] = jnp.transpose(jnp.concatenate([pair_code, pair_code], axis=0))
        slots = lax.broadcasted_iota(jnp.int32, (1, chunk), 1) + at
        staying = (dest_ref[:, here] == my_slab) & (slots < live)
        stay_rows = jnp.broadcast_to(jnp.where(staying, 1.0, 0.0), (part, chunk))
        keep_t[...] = jnp.transpose(stay_rows)
        inverse_t[...] = inverse_order(order_ref[here, :])

        order = order_ref[here, :]
        inverse = inverse_t[...]
        partner = take_lanes(order, inverse ^ pairs)
        code = take_lanes(packed_t[...], inverse & (pairs - 1))
        taken = code >= NDIR
        turn = code & (NDIR - 1)
        low_index = turn & (part - 1)
        is_high = turn >= part
        wide = (chunk, part)
        tables = [jnp.broadcast_to(table[k, 0:1, :], wide) for k in range(4)]
        unit_x = jnp.where(is_high, take_lanes(tables[1], low_index), take_lanes(tables[0], low_index))
        unit_y = jnp.where(is_high, take_lanes(tables[3], low_index), take_lanes(tables[2], low_index))
        unit_z = 1.0 - (2.0 * turn.astype(jnp.float32) + 1.0) / NDIR
        old = [part_ref[3 + k, here, :] for k in range(3)]
        other = [take_lanes(v, partner) for v in old]
        relative = [a - b for a, b in zip(old, other)]
        speed = jnp.sqrt(relative[0] * relative[0] + relative[1] * relative[1] + relative[2] * relative[2])
        half_speed = jnp.where(inverse < pairs, 0.5, -0.5) * speed
        new = [
            jnp.where(taken, 0.5 * (a + b) + half_speed * u, a)
            for a, b, u in zip(old, other, (unit_x, unit_y, unit_z))
        ]
        keep = keep_t[...] > 0.0
        target = pl.ds(pl.multiple_of(MOVE + at, chunk), chunk)
        square[here, :] = new[0] * new[0] + new[1] * new[1] + new[2] * new[2]
        for k in range(3):
            moved_ref[k, target, :] = jnp.where(keep, part_ref[k, here, :] + TIME_STEP * new[k], 0.0)
            moved_ref[3 + k, target, :] = jnp.where(keep, new[k], 0.0)
            for j, piece in enumerate(split3(new[k])):
                parts[j, here, pl.ds(k * part, part)] = piece

        @pl.when((step == 0) & is_end)
        def _():
            pl.semaphore_wait(far_sem, 1)
            start(place_far)

        return carry

    lax.fori_loop(0, steps, chunk_step, 0)

    for k in range(3):
        sent = pick_rows(chosen_ref[...], [parts[j, :, pl.ds(k * part, part)] for j in range(2)])
        sent_speed[0, k] = sent[:MOVE]
        sent_speed[1, k] = sent[MOVE:]

        @pl.when(jnp.logical_not(is_first))
        def _(k=k):
            speed_far[k].start()

        @pl.when(jnp.logical_not(is_end))
        def _(k=k):
            speed_near[k].start()

    @pl.when(is_end)
    def _():
        start(speed_near)

    @pl.when(is_first)
    def _():
        start(speed_far)

    cell_load.wait()
    living = lax.broadcasted_iota(jnp.int32, (1, cap), 1) < live
    ones = jnp.ones((8, part), jnp.bfloat16)
    eight = lax.broadcasted_iota(jnp.int32, (8, cap), 0)
    terms = []
    for k in range(3):
        here = pl.ds(k * part, part)
        terms.append(dot_nt(ones, parts[0, :, here]) + dot_nt(ones, parts[1, :, here]) + dot_nt(ones, parts[2, :, here]))
    pieces = split3(square[...])
    terms.append(dot_nt(ones, pieces[0]) + dot_nt(ones, pieces[1]) + dot_nt(ones, pieces[2]))
    term = jnp.where(eight == 0, terms[0], jnp.where(eight == 1, terms[1], jnp.where(eight == 2, terms[2], terms[3])))
    term = jnp.where(living, term, 0.0)
    shifted = cell_ref[...] + (CELLS - my_rep * share)
    shifted = jnp.where(shifted >= CELLS, shifted - CELLS, shifted)
    cells = lax.broadcasted_iota(jnp.int32, (CELLS, cap), 0)
    in_cell = jnp.where(cells == shifted, 1.0, 0.0).astype(jnp.bfloat16)
    high, middle_part, low = split3(term)
    total = dot_nt(high, in_cell) + dot_nt(middle_part, in_cell) + dot_nt(low, in_cell)
    for j in range(reps):
        sent_cells[j] = total[0:4, j * share:(j + 1) * share]
    start(cell_copies)

    total = sent_cells[0]
    for k in range(1, reps):
        cell_copies[k - 1].wait()
        total = total + got_cells[k]
    samples_ref[...] = total / (part * reps)
    for k in range(3):
        for j, at in ((0, 0), (1, MOVE + cap)):
            target = pl.ds(at, MOVE)
            for base, sent, got in ((0, sent_place, got_place), (6, sent_speed, got_speed)):
                copy(sent.at[j, k], got.at[j, k], base + 3 * j + k, {"space": near_slab}).wait_recv()
            moved_ref[k, target, :] = got_place[j, k] + TIME_STEP * got_speed[j, k]
            moved_ref[3 + k, target, :] = got_speed[j, k]
    for each in place_far + place_near + speed_far + speed_near:
        each.wait_send()


def assemble_kernel(held_ref, cells_ref, moved_ref, samples_ref, sems):
    copies = [
        pltpu.make_async_copy(held_ref, moved_ref, sems.at[0]),
        pltpu.make_async_copy(cells_ref, samples_ref, sems.at[1]),
    ]
    for each in copies:
        each.start()
    for each in copies:
        each.wait()


def per_device(particles, pair_order, accepted, direction, destination, live_count, cell_index):
    six, _, cap, part = particles.shape
    three = six // 2
    pairs = accepted.shape[2]
    chunk = MOVE
    slabs = lax.axis_size("space")
    reps = lax.axis_size("rep")
    share = CELLS // reps
    f32 = jnp.float32
    out_cap = cap + 2 * MOVE
    in_vmem = pl.BlockSpec(memory_space=pltpu.VMEM)
    in_hbm = pl.BlockSpec(memory_space=pltpu.HBM)
    movers = pltpu.VMEM((2, three, MOVE, part), f32)
    outs = [
        jax.ShapeDtypeStruct((six, out_cap, part), f32),
        jax.ShapeDtypeStruct((4, share), f32),
    ]
    call = pl.pallas_call(
        functools.partial(main_kernel, slabs),
        in_specs=[in_hbm] * 5 + [pl.BlockSpec(memory_space=pltpu.SMEM), in_hbm],
        out_specs=[in_vmem] * 2,
        out_shape=outs,
        scratch_shapes=[
            pltpu.VMEM((six, cap, part), f32),
            pltpu.VMEM((cap, part), jnp.int32),
            pltpu.VMEM((pairs, cap), jnp.int32),
            pltpu.VMEM((pairs, cap), jnp.int32),
            pltpu.VMEM((1, cap), jnp.int32),
            pltpu.VMEM((1, cap), jnp.int32),
            pltpu.VMEM((4, 8, part), f32),
            pltpu.VMEM((chunk, part), jnp.int32),
            pltpu.VMEM((chunk, part), f32),
            pltpu.VMEM((chunk, part), jnp.int32),
            pltpu.VMEM((3, cap, three * part), jnp.bfloat16),
            pltpu.VMEM((cap, part), f32),
            pltpu.VMEM((2 * MOVE, cap), jnp.bfloat16),
            movers,
            movers,
            movers,
            movers,
            pltpu.VMEM((reps, 4, share), f32),
            pltpu.VMEM((reps, 4, share), f32),
            pltpu.SemaphoreType.DMA((9,)),
            pltpu.SemaphoreType.DMA((11 + reps,)),
            pltpu.SemaphoreType.DMA((11 + reps,)),
            pltpu.SemaphoreType.REGULAR,
        ],
        compiler_params=pltpu.CompilerParams(collective_id=0, has_side_effects=True, vmem_limit_bytes=16 * 2 ** 20),
        name="step",
    )
    operands = (
        particles.reshape(six, cap, part),
        pair_order.reshape(cap, part),
        jnp.transpose(accepted.reshape(cap, pairs)),
        jnp.transpose(direction.reshape(cap, pairs)),
        destination.reshape(1, cap),
        live_count,
        cell_index.reshape(1, cap),
    )
    hold = functools.partial(pltpu.with_memory_space_constraint, memory_space=pltpu.HBM)
    operands = [x if x is live_count else hold(x) for x in operands]
    moved, samples = pl.pallas_call(
        assemble_kernel,
        in_specs=[in_vmem] * 2,
        out_specs=[in_hbm] * 2,
        out_shape=outs,
        scratch_shapes=[pltpu.SemaphoreType.DMA((2,))],
        compiler_params=pltpu.CompilerParams(vmem_limit_bytes=2 * 2 ** 20),
        name="assemble",
    )(*call(*operands))
    return (moved[:, None], samples[:, None, :])


def solution(mesh):
    return jax.shard_map(
        per_device,
        mesh=mesh,
        in_specs=(
            P(None, "rep", "space", None),
            P("rep", "space", None),
            P("rep", "space", None),
            P("rep", "space", None),
            P("rep", "space"),
            P("rep", "space"),
            P("rep", "space"),
        ),
        out_specs=(P(None, "rep", "space", None), P(None, "space", "rep")),
        check_vma=False,
    )
```

time: 26.9 us -> 23.6 us (0.88)
  the two profiles are of different devices: /device:TPU:0 before, /device:TPU:29 now
where the time goes in v1:
time: 23.6 us; the launch traced here: 23.5 us
  Pallas kernels  22.2 us (94%)
  between operations  1.29 us (5%)
    pallas_call x1, Pallas kernels, per_device(): call(*operands)  20.7 us
    pallas_call x1, Pallas kernels, per_device(): pl.pallas_call(assemble_kernel, in_specs=[in_vmem] * 2, out_specs=[in_hbm...  1.43 us

profile of v1, /device:TPU:29, one launch (start us, length us, event | category | flops | bytes accessed | tf_op | source)
XLA Modules:
  0.0 23.5 jit_solution(9688797744860151621)
XLA Ops:
  1.3 20.7 %step.1 = (f32[6,768,128]{2,1,0:T(8,128)S(1)}, f32[4,128]{1,0:T(4,128)S(1)}) custom-call(f32[6,512,128]{2,1,0:T(8,128)} %bitcast.14, s32[512,128]{1,0:T(8,128)} %bitcast.15, s32[64,512]{1,0:T(8,128)} %bitcast.16, s32[64,512]{1,0:T(8,128)} %bitcast.17, s32[1,512]{1,0:T(1,128)} %dest_hbm.1, s32[1,1]{1,0:T(1,128)S(6)} %copy.11.live_ref, s32[1,512]{1,0:T(1,128)} %cell_hbm.1), custom_call_target="tpu_custom_call" | custom-call | tf_op jit(solution)/shard_map/step/pallas_call | solution.py:426
  22.0 1.4 %assemble.1 = (f32[6,768,128]{2,1,0:T(8,128)}, f32[4,128]{1,0:T(4,128)}) custom-call(f32[6,768,128]{2,1,0:T(8,128)S(1)} %get-tuple-element.6.held_ref, f32[4,128]{1,0:T(4,128)S(1)} %get-tuple-element.7.cells_ref), custom_call_target="tpu_custom_call" | custom-call | tf_op jit(solution)/shard_map/assemble/pallas_call | solution.py:418

commit v2 on v1

--- a/solution.py
+++ b/solution.py
@@ -12,6 +12,10 @@
 CELLS = 256
 TIME_STEP = 0.25
 GOLDEN_TURN = 2.399963229728653
+FAR_STEP = 2
+PLACE_GROUPS = ((0, 1), (1, 2))
+FAR_GROUPS = ((0, 3),)
+NEAR_GROUPS = ((0, 3),)
 
 
 def take_lanes(values, index):
@@ -129,8 +133,10 @@
     far_slab = lax.rem(my_slab + slabs - 1 + 2 * odd, slabs)
     goals = (lax.rem(my_slab + 1, slabs), lax.rem(my_slab + slabs - 1, slabs))
     is_end = (my_slab == 0) | (my_slab == slabs - 1)
-    middle = slabs // 2 - 1
-    is_middle = my_slab == middle
+    assert slabs % 4 == 0
+    quarter = lax.rem(my_slab, 4)
+    is_hub = quarter == 2
+    is_last = my_slab == 0
     is_first = my_slab == 1
     live = live_ref[0, 0]
 
@@ -156,13 +162,15 @@
             device_id=device, device_id_type=pl.DeviceIdType.MESH,
         )
 
-    def mover_copies(sent, got, base, j, device):
-        return [copy(sent.at[j, k], got.at[j, k], base + 3 * j + k, {"space": device}) for k in range(3)]
-
-    place_far = mover_copies(sent_place, got_place, 0, far, far_slab)
-    place_near = mover_copies(sent_place, got_place, 0, near, near_slab)
-    speed_far = mover_copies(sent_speed, got_speed, 6, far, far_slab)
-    speed_near = mover_copies(sent_speed, got_speed, 6, near, near_slab)
+    def mover_copies(sent, got, base, j, device, groups):
+        return [
+            copy(sent.at[j, pl.ds(k, n)], got.at[j, pl.ds(k, n)], base + 3 * j + k, {"space": device}) for k, n in groups
+        ]
+
+    place_far = mover_copies(sent_place, got_place, 0, far, far_slab, PLACE_GROUPS)
+    place_near = mover_copies(sent_place, got_place, 0, near, near_slab, PLACE_GROUPS)
+    speed_far = mover_copies(sent_speed, got_speed, 6, far, far_slab, FAR_GROUPS)
+    speed_near = mover_copies(sent_speed, got_speed, 6, near, near_slab, NEAR_GROUPS)
     cell_copies = [
         copy(sent_cells.at[k], got_cells.at[k], 11 + k, {"rep": lax.rem(my_rep + k, reps)}) for k in range(1, reps)
     ]
@@ -180,11 +188,11 @@
     for k in range(1, reps):
         greet(rep=lax.rem(my_rep + k, reps))
 
-    @pl.when(is_end)
-    def _():
-        greet(space=middle)
-
-    @pl.when(jnp.logical_not(is_end))
+    @pl.when(quarter == 0)
+    def _():
+        greet(space=lax.rem(my_slab + slabs - 2, slabs))
+
+    @pl.when(quarter == 1)
     def _():
         greet(space=far_slab)
 
@@ -196,29 +204,23 @@
         sent_place[0, k] = sent[:MOVE]
         sent_place[1, k] = sent[MOVE:]
         if k == 0:
-            @pl.when(is_end)
+            @pl.when(is_hub)
+            def _():
+                pl.semaphore_wait(barrier, 2 + reps)
+                for other in (near_slab, far_slab, lax.rem(my_slab + 2, slabs)):
+                    pl.semaphore_signal(far_sem, inc=1, device_id={"space": other}, device_id_type=pl.DeviceIdType.MESH)
+
+            @pl.when(jnp.logical_not(is_hub))
             def _():
                 pl.semaphore_wait(barrier, reps)
 
-            @pl.when(is_middle)
-            def _():
-                pl.semaphore_wait(barrier, 3 + reps)
-                for end in (0, slabs - 1):
-                    pl.semaphore_signal(far_sem, inc=1, device_id={"space": end}, device_id_type=pl.DeviceIdType.MESH)
-
-            @pl.when(jnp.logical_not(is_end | is_middle))
-            def _():
-                pl.semaphore_wait(barrier, 1 + reps)
-
-        @pl.when(jnp.logical_not(is_end | is_first))
-        def _(k=k):
-            place_far[k].start()
-
-        place_near[k].start()
-
-        @pl.when(is_first)
-        def _(k=k):
-            place_far[k].start()
+        for i, (first, count) in enumerate(PLACE_GROUPS):
+            if first + count == k + 1:
+                place_near[i].start()
+
+                @pl.when(is_hub)
+                def _(i=i):
+                    place_far[i].start()
 
     for half in range(2):
         turns = (lax.broadcasted_iota(jnp.int32, (8, part), 1) + half * part).astype(jnp.float32)
@@ -275,7 +277,7 @@
             for j, piece in enumerate(split3(new[k])):
                 parts[j, here, pl.ds(k * part, part)] = piece
 
-        @pl.when((step == 0) & is_end)
+        @pl.when((step == jnp.where(is_last, steps - 1, FAR_STEP)) & jnp.logical_not(is_hub))
         def _():
             pl.semaphore_wait(far_sem, 1)
             start(place_far)
@@ -289,17 +291,11 @@
         sent_speed[0, k] = sent[:MOVE]
         sent_speed[1, k] = sent[MOVE:]
 
-        @pl.when(jnp.logical_not(is_first))
-        def _(k=k):
-            speed_far[k].start()
-
-        @pl.when(jnp.logical_not(is_end))
-        def _(k=k):
-            speed_near[k].start()
-
-    @pl.when(is_end)
-    def _():
-        start(speed_near)
+    @pl.when(jnp.logical_not(is_first))
+    def _():
+        start(speed_far)
+
+    start(speed_near)
 
     @pl.when(is_first)
     def _():
@@ -332,13 +328,29 @@
         cell_copies[k - 1].wait()
         total = total + got_cells[k]
     samples_ref[...] = total / (part * reps)
-    for k in range(3):
-        for j, at in ((0, 0), (1, MOVE + cap)):
-            target = pl.ds(at, MOVE)
-            for base, sent, got in ((0, sent_place, got_place), (6, sent_speed, got_speed)):
-                copy(sent.at[j, k], got.at[j, k], base + 3 * j + k, {"space": near_slab}).wait_recv()
-            moved_ref[k, target, :] = got_place[j, k] + TIME_STEP * got_speed[j, k]
-            moved_ref[3 + k, target, :] = got_speed[j, k]
+    for k, n in PLACE_GROUPS:
+        for j in range(2):
+            here = pl.ds(k, n)
+            copy(sent_place.at[j, here], got_place.at[j, here], 3 * j + k, {"space": near_slab}).wait_recv()
+
+    def take(base, groups, j):
+        for k, n in groups:
+            here = pl.ds(k, n)
+            copy(sent_speed.at[j, here], got_speed.at[j, here], 6 + 3 * j + k, {"space": near_slab}).wait_recv()
+            for i in range(k, k + n):
+                moved_ref[i, pl.ds(base, MOVE), :] = got_place[j, i] + TIME_STEP * got_speed[j, i]
+                moved_ref[3 + i, pl.ds(base, MOVE), :] = got_speed[j, i]
+
+    @pl.when(odd == 0)
+    def _():
+        take(0, FAR_GROUPS, 0)
+        take(MOVE + cap, NEAR_GROUPS, 1)
+
+    @pl.when(odd == 1)
+    def _():
+        take(MOVE + cap, FAR_GROUPS, 1)
+        take(0, NEAR_GROUPS, 0)
+
     for each in place_far + place_near + speed_far + speed_near:
         each.wait_send()
 

time: 23.6 us -> 23.6 us (level)
  the two profiles are of different devices: /device:TPU:29 before, /device:TPU:0 now
where the time goes in v2:
time: 23.6 us; the launch traced here: 23.5 us
  Pallas kernels  22.2 us (94%)
  between operations  1.29 us (5%)
    pallas_call x1, Pallas kernels, per_device(): call(*operands)  20.7 us
    pallas_call x1, Pallas kernels, per_device(): pl.pallas_call(assemble_kernel, in_specs=[in_vmem] * 2, out_specs=[in_hbm...  1.43 us

profile of v2, /device:TPU:0, one launch (start us, length us, event | category | flops | bytes accessed | tf_op | source)
XLA Modules:
  0.0 23.5 jit_solution(2007506716722228184)
XLA Ops:
  1.3 20.7 %step.1 = (f32[6,768,128]{2,1,0:T(8,128)S(1)}, f32[4,128]{1,0:T(4,128)S(1)}) custom-call(f32[6,512,128]{2,1,0:T(8,128)} %bitcast.14, s32[512,128]{1,0:T(8,128)} %bitcast.15, s32[64,512]{1,0:T(8,128)} %bitcast.16, s32[64,512]{1,0:T(8,128)} %bitcast.17, s32[1,512]{1,0:T(1,128)} %dest_hbm.1, s32[1,1]{1,0:T(1,128)S(6)} %copy.11.live_ref, s32[1,512]{1,0:T(1,128)} %cell_hbm.1), custom_call_target="tpu_custom_call" | custom-call | tf_op jit(solution)/shard_map/step/pallas_call | solution.py:438
  22.0 1.4 %assemble.1 = (f32[6,768,128]{2,1,0:T(8,128)}, f32[4,128]{1,0:T(4,128)}) custom-call(f32[6,768,128]{2,1,0:T(8,128)S(1)} %get-tuple-element.6.held_ref, f32[4,128]{1,0:T(4,128)S(1)} %get-tuple-element.7.cells_ref), custom_call_target="tpu_custom_call" | custom-call | tf_op jit(solution)/shard_map/assemble/pallas_call | solution.py:430
